TPU v7x, 32 devices: a whole 2x2x4 slice. The times are simulated.
32 devices in a mesh: groups: 2 (over y), replay: 4 (over z), module: 2 (over x), half: 2 (over core).
Axes of the slice: x: 2, y: 2, z: 4, core: 2. Of those that a mesh axis runs over, the one named last changes fastest.
Arguments:
- new_factors: bfloat16 [128, 2, 64, 128], P(('groups', 'replay', 'module')), parts along dimension 0, may hold values from -0.5 to 0.5
- new_counts: int32 [128], P(('groups', 'replay', 'module')), parts along dimension 0, may hold values from 32 to 64
- new_ids: int32 [128], P(('groups', 'module', 'half')), parts along dimension 0, may hold values from 0 to 3071
- replay_grads: bfloat16 [6144, 2, 4096], P(('groups', 'replay'), 'module', 'half'), parts along dimension 0, may hold values from -0.75 to 0.75
- replay_ids: int32 [6144], P(('groups', 'replay')), parts along dimension 0, may hold values from 0 to 3071
- slot_module: int32 [2], replicated, may hold values from 0 to 1, each once
- output_inverse: float32 [2, 64, 64], replicated, as said below
- input_inverse: float32 [2, 64, 64], replicated, as said below
Outputs:
- scores: float32 [128, 3072], P(('groups', 'module', 'half'), 'replay'), parts along dimension 0
There are 2 independent parts, one for each index of `groups`. A program takes and returns all parts, laid end to end along the dimension named above; an argument that names none is the same for every part. Nothing has to cross between parts.
Inputs may be any that keep to these rules, and one draw needn't show every extreme that they name: `new_counts`: each new example has at least half of its token slots live, the live ones first. `slot_module`: each module sits in exactly one slot. `output_inverse`: symmetric with a positive diagonal. `input_inverse`: symmetric with a positive diagonal.
All inputs are finite; a program needn't handle non-finite values.
Results may differ from a plain program's by a relative error of at most 0.0029.
Values may be sent and summed in bfloat16 or wider, within the bound.
A program may use at most 64 MiB of HBM per device.

v0:
```python
import jax
import jax.numpy as jnp
from jax import lax
from jax.sharding import PartitionSpec as P


def body(
    new_factors,
    new_counts,
    new_ids,
    replay_grads,
    replay_ids,
    slot_module,
    output_inverse,
    input_inverse,
):
    module_count = output_inverse.shape[0]
    feature_count = output_inverse.shape[1]
    token_count = new_factors.shape[2]
    row_share = replay_grads.shape[2] // feature_count
    token_index = lax.iota(jnp.int32, token_count)
    token_live = token_index[None, :] < new_counts[:, None]
    live_factors = jnp.where(token_live[:, None, :, None], new_factors, jnp.zeros((), jnp.bfloat16))
    selector = slot_module[:, None] == lax.iota(jnp.int32, module_count)[None, :]
    slot_factors = jnp.einsum(
        "sm,emtc->estc",
        selector.astype(jnp.bfloat16),
        live_factors,
        preferred_element_type=jnp.float32,
    ).astype(jnp.bfloat16)
    left_inverse = jnp.einsum(
        "sm,mrc->src", selector.astype(jnp.float32), output_inverse, precision=lax.Precision.HIGHEST
    )
    right_inverse = jnp.einsum(
        "sm,mrc->src", selector.astype(jnp.float32), input_inverse, precision=lax.Precision.HIGHEST
    )
    first_row = lax.axis_index("half") * row_share
    left_rows = lax.dynamic_slice_in_dim(left_inverse, first_row, row_share, 1)
    activations = slot_factors[:, :, :, :feature_count]
    output_grads = slot_factors[:, :, :, feature_count:]
    gradients = jnp.einsum(
        "estr,estc->esrc", output_grads, activations, preferred_element_type=jnp.float32
    )
    preconditioned = jnp.einsum(
        "srk,eskc->esrc", left_rows, gradients, precision=lax.Precision.HIGHEST
    )
    preconditioned = jnp.einsum(
        "esrk,skc->esrc", preconditioned, right_inverse, precision=lax.Precision.HIGHEST
    )
    local_rows = preconditioned.astype(jnp.bfloat16).reshape(
        preconditioned.shape[0], module_count, row_share * feature_count
    )
    regrouped = lax.all_to_all(local_rows, "module", split_axis=1, concat_axis=0, tiled=True)
    new_block = regrouped.reshape(regrouped.shape[0], -1)
    replay_rows = replay_grads.reshape(replay_grads.shape[0], -1)
    partials = lax.dot_general(
        lax.all_gather(new_block, "replay", axis=0, tiled=True),
        replay_rows,
        (((1,), (1,)), ((), ())),
        preferred_element_type=jnp.float32,
    )
    summed_scores = lax.psum_scatter(partials, ("module", "half"), scatter_dimension=0, tiled=True)
    self_pairs = new_ids[:, None] == replay_ids[None, :]
    return jnp.where(self_pairs, jnp.zeros((), jnp.float32), summed_scores)


def solution(mesh):
    in_specs = (
        P(("groups", "replay", "module"), None, None, None),
        P(("groups", "replay", "module")),
        P(("groups", "module", "half")),
        P(("groups", "replay"), "module", "half"),
        P(("groups", "replay")),
        P(),
        P(),
        P(),
    )
    out_specs = P(("groups", "module", "half"), "replay")
    return jax.shard_map(body, mesh=mesh, in_specs=in_specs, out_specs=out_specs, check_vma=False)
```

profile of v0, /device:TPU:0, one launch (start us, length us, event | category | flops | bytes accessed | tf_op | source)
XLA Modules:
  0.0 69.8 jit_solution(8169205786504913018)
XLA Ops:
  6.5 0.0 copy-start
  6.5 0.0 reduce-scatter.2.cloned.1.call-start
  6.5 0.9 %iota_compare_fusion = pred[8,64]{1,0:T(8,128)(4,1)S(1)} fusion(s32[8]{0:T(128)} %param.9), kind=kLoop, calls=%fused_computation.20 | loop fusion | flops 512 | bytes 544 | tf_op jit(solution)/shard_map/lt | solution.py:22
  7.4 1.2 %broadcast_select_fusion = bf16[8,2,64,128]{3,2,1,0:T(8,128)(2,1)S(1)} fusion(bf16[8,2,64,128]{3,2,1,0:T(8,128)(2,1)} %param.8, pred[8,64]{1,0:T(8,128)(4,1)S(1)} %iota_compare_fusion), kind=kLoop, calls=%fused_computation.12 | loop fusion | flops 131072 | bytes 524800 | tf_op jit(solution)/shard_map/jit(_where)/select_n | solution.py:23
  8.6 1.1 %fusion.2 = bf16[8,2,64,128]{3,1,2,0:T(2,128)(2,1)S(1)} fusion(bf16[8,2,64,128]{3,2,1,0:T(8,128)(2,1)S(1)} %broadcast_select_fusion, s32[2]{0:T(128)} %param.13), kind=kOutput, calls=%fused_computation.3 | convolution fusion | flops 655364 | bytes 524296 | tf_op jit(solution)/shard_map/sm,emtc->estc/dot_general | solution.py:25
  9.7 1.2 %fusion.19 = (bf16[8,2,64,64]{3,1,2,0:T(2,128)(2,1)S(1)}, bf16[8,2,64,64]{3,1,2,0:T(2,128)(2,1)}) fusion(bf16[8,2,64,128]{3,1,2,0:T(2,128)(2,1)S(1)} %fusion.2), kind=kLoop, calls=%fused_computation.29 | loop fusion | bytes 524288 | tf_op jit(solution)/shard_map/slice | solution.py:40
  10.9 1.2 %fusion.10 = f32[2,64,64]{2,0,1:T(2,128)S(1)} fusion(f32[2,64,64]{2,1,0:T(8,128)} %param.14, s32[2]{0:T(128)} %param.13), kind=kOutput, calls=%fused_computation.15 | convolution fusion | flops 196612 | bytes 65544 | tf_op jit(solution)/shard_map/sm,mrc->src/dot_general | solution.py:31
  12.1 1.2 %convolution_bitcast_fusion.1 = f32[2,64,64,1]{2,0,1,3:T(2,128)S(1)} fusion(f32[2,64,64]{2,1,0:T(8,128)} %param.15, s32[2]{0:T(128)} %param.13), kind=kOutput, calls=%fused_computation.7 | convolution fusion | flops 196612 | bytes 65544 | tf_op jit(solution)/shard_map/sm,mrc->src/dot_general | solution.py:34
  13.3 2.0 %fusion.5 = f32[8,2,64,64]{3,2,1,0:T(8,128)} fusion(bf16[8,2,64,64]{3,1,2,0:T(2,128)(2,1)} %get-tuple-element.6, bf16[8,2,64,64]{3,1,2,0:T(2,128)(2,1)S(1)} %get-tuple-element.5), kind=kOutput, calls=%fused_computation.9 | convolution fusion | flops 8388608 | bytes 524288 | tf_op jit(solution)/shard_map/estr,estc->esrc/dot_general | solution.py:41
  15.3 0.0 copy-start.1
  15.3 0.0 copy-start.2
  15.3 1.5 %convolution_bitcast_fusion = f32[8,2,32,64]{3,2,0,1:T(8,128)S(1)} fusion(f32[8,2,64,64]{3,2,1,0:T(8,128)} %fusion.5, f32[2,32,64]{2,0,1:T(2,128)S(1)} %constant_dynamic-slice_fusion), kind=kOutput, calls=%fused_computation.4 | convolution fusion | flops 25165824 | bytes 409600 | tf_op jit(solution)/shard_map/srk,eskc->esrc/dot_general | solution.py:44
  16.8 0.4 fusion.3
  17.1 0.2 reshape.33
  17.3 8.2 %all_to_all.15 = bf16[8,2,2048]{2,0,1:T(8,128)(2,1)S(1)} all-to-all(bf16[8,2,2048]{2,0,1:T(8,128)(2,1)S(1)} %reshape.33), channel_id=1, replica_groups=mesh['groups'=2,'replay'=4,'module'=2,'half'=2] {'module'}, dimensions={1} | all-to-all | bytes 131072 | tf_op jit(solution)/shard_map/all_to_all | solution.py:53
  25.5 14.1 %all_gather.3 = bf16[64,2048]{1,0:T(8,128)(2,1)S(1)} all-gather(bf16[16,2048]{1,0:T(8,128)(2,1)S(1)} %bitcast.37), channel_id=1, replica_groups=mesh['groups'=2,'replay'=4,'module'=2,'half'=2] {'replay'}, dimensions={0}, use_global_device_ids=true | all-gather | bytes 327680 | tf_op jit(solution)/shard_map/all_gather | solution.py:57
  39.6 0.0 copy-done
  39.6 1.7 %fusion = f32[64,768]{1,0:T(8,128)} fusion(bf16[64,2048]{1,0:T(8,128)(2,1)S(1)} %all_gather.3, bf16[768,1,2048]{2,0,1:T(8,128)(2,1)S(1)} %copy-done), kind=kOutput, calls=%fused_computation | convolution fusion | flops 201326592 | bytes 3604480 | tf_op jit(solution)/shard_map/dot_general | solution.py:56
  41.4 0.0 reduce-scatter.2.cloned.1.call-update
  41.4 20.1 %reduce-scatter.2.cloned.1.call-done = f32[16,768]{1,0:T(8,128)} async-done(((f32[64,768]{1,0:T(8,128)}), f32[16,768]{1,0:T(8,128)}) %reduce-scatter.2.cloned.1.call-update) | async-done | bytes 49168 | tf_op jit(solution)/shard_map/reduce_scatter | solution.py:62
  61.5 0.0 copy-done.1
  61.5 0.0 copy-done.2
  61.5 1.5 %compare_select_fusion = f32[16,768]{1,0:T(8,128)} fusion(f32[16,768]{1,0:T(8,128)} %reduce-scatter.2.cloned.1.call-done, s32[768]{0:T(1024)S(1)} %copy-done.1, s32[16]{0:T(128)S(1)} %copy-done.2), kind=kLoop, calls=%fused_computation.18 | loop fusion | flops 24576 | bytes 101440 | tf_op jit(solution)/shard_map/jit(_where)/select_n | solution.py:64
  (1 shorter events, 0.0 us)
Async XLA Ops:
  6.5 33.1 %copy-start = (bf16[768,1,2048]{2,0,1:T(8,128)(2,1)S(1)}, bf16[768,1,2048]{2,0,1:T(8,128)(2,1)}, u32[]{:S(2)}) copy-start(bf16[768,1,2048]{2,0,1:T(8,128)(2,1)} %param.11) | copy-start | bytes 9437188
  6.5 54.9 %reduce-scatter.2.cloned.1.call-start = ((), (), s32[]{:S(2)}) async-start(), calls=%async_computation.2 | async-start | bytes 245760 | tf_op jit(solution)/shard_map/reduce_scatter | solution.py:62
  15.3 46.2 %copy-start.1 = (s32[768]{0:T(1024)S(1)}, s32[768]{0:T(1024)}, u32[]{:S(2)}) copy-start(s32[768]{0:T(1024)} %param.12) | copy-start | bytes 9220
  15.3 46.2 %copy-start.2 = (s32[16]{0:T(128)S(1)}, s32[16]{0:T(128)}, u32[]{:S(2)}) copy-start(s32[16]{0:T(128)} %param.10) | copy-start | bytes 196
Sparse Core Ops, SparseCore 0:
  41.5 19.9 reduce-scatter.1
where the time goes:
time: 70.2 us; the launch traced here: 69.8 us
  blocking collectives  22.3 us (32%)
  waiting for transfers between devices  20.1 us (29%)
  between operations  13.5 us (19%)
  matrix products  9.07 us (13%)
  other arithmetic  3.53 us (5%)
  local copies, waits for them, and re-layouts  1.37 us (2%)
    reduce_scatter x1, waiting for transfers between devices, body(): lax.psum_scatter(partials, ('module', 'half'), scatter_dimension=0, tiled...  20.1 us
    all_gather x1, blocking collectives, body(): lax.all_gather(new_block, 'replay', axis=0, tiled=True)  14.1 us
    all_to_all x1, blocking collectives, body(): lax.all_to_all(local_rows, 'module', split_axis=1, concat_axis=0, tiled=T...  8.16 us
    dot_general x1, matrix products, body(): jnp.einsum('estr,estc->esrc', output_grads, activations, preferred_elemen...  2.02 us
    dot_general x1, matrix products, body(): lax.dot_general(lax.all_gather(new_block, 'replay', axis=0, tiled=True),...  1.75 us
    select_n x1, other arithmetic, body(): return jnp.where(self_pairs, jnp.zeros((), jnp.float32), summed_scores)  1.49 us
    dot_general x1, matrix products, body(): jnp.einsum('srk,eskc->esrc', left_rows, gradients, precision=lax.Precisio...  1.47 us
  transfers between devices with their start and end apart: 1, of which 1 were waited for; matrix products, arithmetic and copies ran while one was open for 0% of the time, Pallas kernels for 0%

commit v1 on v0

v1 whole, which is shorter than its diff:
```python
import functools

import jax
import jax.numpy as jnp
from jax import lax
from jax.experimental import pallas as pl
from jax.experimental.pallas import tpu as pltpu
from jax.sharding import PartitionSpec as P

MESH = pl.DeviceIdType.MESH
UNROLL = 16


def each(count, step):
    if count <= UNROLL:
        for index in range(count):
            step(index)
    else:
        def one(index, carry):
            step(index)
            return carry

        lax.fori_loop(0, count, one, 0)


def parts_of(value):
    high = value.astype(jnp.bfloat16)
    low = (value - high.astype(jnp.float32)).astype(jnp.bfloat16)
    return high, low


def kernel(
    sizes,
    slot_module,
    counts,
    factors_hbm,
    replay_hbm,
    left_hbm,
    right_hbm,
    out_ref,
    factors,
    replay,
    left,
    right,
    rows_f32,
    outgoing,
    blocks,
    part,
    arrived,
    load_sem,
    send_sem,
    recv_sem,
    score_send_sem,
    score_recv_sem,
):
    replays, modules, halves, chunk = sizes
    z, x, h = lax.axis_index("replay"), lax.axis_index("module"), lax.axis_index("half")
    block = z * modules + x
    owner = x * halves + h
    owners = modules * halves
    examples, _, tokens, width = factors.shape
    feat = width // 2
    share = replay.shape[1] // feat
    columns = replay.shape[0]
    chunks = columns // chunk

    small_loads = [
        pltpu.make_async_copy(factors_hbm, factors, load_sem.at[0]),
        pltpu.make_async_copy(left_hbm, left, load_sem.at[1]),
        pltpu.make_async_copy(right_hbm, right, load_sem.at[2]),
    ]
    for load in small_loads:
        load.start()
    replay_load = pltpu.make_async_copy(replay_hbm, replay, load_sem.at[3])
    replay_load.start()

    barrier = pltpu.get_barrier_semaphore()

    def greet_block(offset):
        target = lax.rem(block + offset + 1, replays * modules)
        pl.semaphore_signal(
            barrier,
            inc=1,
            device_id={"replay": target // modules, "module": lax.rem(target, modules)},
            device_id_type=MESH,
        )

    def greet_owner(offset):
        index = lax.rem(h + offset % (halves - 1) + 1, halves)
        pl.semaphore_signal(
            barrier,
            inc=1,
            device_id={"module": offset // (halves - 1), "half": index},
            device_id_type=MESH,
        )

    each(replays * modules - 1, greet_block)
    for offset in range(modules * (halves - 1)):
        greet_owner(offset)

    for load in small_loads:
        load.wait()

    pair = 128 // tokens
    lane = lax.broadcasted_iota(jnp.int32, (share, 128), 1)
    zero = jnp.zeros((), jnp.bfloat16)
    low_lanes = lax.broadcasted_iota(jnp.int32, (examples, 2 * feat), 1) < feat

    def precondition(slot):
        module = slot_module[slot]
        entries = factors[:, module].reshape(examples * tokens, width)
        doubled = jnp.concatenate([entries, entries], axis=1)
        right_high, right_low = parts_of(right[module])
        blank = jnp.zeros((feat, feat), jnp.bfloat16)
        right_rows = jnp.concatenate([right_high, blank, right_low, blank], axis=0)
        right_rows = jnp.concatenate([right_rows, right_rows], axis=1)
        v = jnp.dot(doubled, right_rows, preferred_element_type=jnp.float32)
        left_high, left_low = parts_of(left[module, pl.ds(pl.multiple_of(h * share, share), share), :])
        left_blank = jnp.zeros((share, feat), jnp.bfloat16)
        left_columns = jnp.concatenate([left_blank, left_high, left_blank, left_low], axis=1)
        u = lax.dot_general(
            left_columns, doubled, (((1,), (1,)), ((), ())), preferred_element_type=jnp.float32
        )
        v_high, v_low = parts_of(v)
        for group in range(examples // pair):
            u_pair = u[:, group * 128 : (group + 1) * 128]
            masked = []
            for inner in range(pair):
                count = counts[group * pair + inner]
                first = inner * tokens
                keep = (lane >= first) & (lane < first + count)
                masked.append(jnp.where(keep, u_pair, 0.0))
            u_high, u_low = parts_of(jnp.concatenate(masked, axis=0))
            lhs = jnp.concatenate([u_high, u_high, u_low], axis=1)
            span = slice(group * 128, (group + 1) * 128)
            rhs = jnp.concatenate([v_high[span], v_low[span], v_high[span]], axis=0)
            rows_f32[pl.ds(group * pair * share, pair * share), :] = jnp.dot(
                lhs, rhs, preferred_element_type=jnp.float32
            )
        for q in range(share // 2):
            even = rows_f32[pl.ds(2 * q, examples, stride=share), :]
            odd = rows_f32[pl.ds(2 * q + 1, examples, stride=share), :]
            outgoing[slot, :, q * 2 * feat : (q + 1) * 2 * feat] = jnp.where(low_lanes, even, odd).astype(
                jnp.bfloat16
            )

    def block_copy(slot, target_z):
        target = target_z * modules + slot
        return pltpu.make_async_remote_copy(
            src_ref=outgoing.at[slot],
            dst_ref=blocks.at[block],
            send_sem=send_sem.at[target],
            recv_sem=recv_sem.at[block],
            device_id={"replay": target_z, "module": slot},
            device_id_type=MESH,
        )

    for step in range(modules):
        slot = lax.rem(x + 1 + step, modules)
        precondition(slot)
        if step == 0:
            pl.semaphore_wait(barrier, replays * modules - 1 + modules * (halves - 1))
        first = 0 if step < modules - 1 else 1
        each(replays - first, lambda index: block_copy(slot, lax.rem(z + first + index, replays)).start())
    blocks[block] = outgoing[x]

    def await_block(offset):
        source = lax.rem(block + offset + 1, replays * modules)
        pltpu.make_async_remote_copy(
            src_ref=outgoing.at[0],
            dst_ref=blocks.at[source],
            send_sem=send_sem.at[source],
            recv_sem=recv_sem.at[source],
            device_id={"replay": source // modules, "module": lax.rem(source, modules)},
            device_id_type=MESH,
        ).wait_recv()

    replay_load.wait()
    each(replays * modules - 1, await_block)

    total = replays * modules * examples
    rows = total // owners
    group_rows = min(total, 256)
    group_blocks = group_rows // examples

    def score_copy(target, c):
        cut = pl.ds(c * chunk, chunk)
        return pltpu.make_async_remote_copy(
            src_ref=part.at[pl.ds(pl.multiple_of(target * rows, rows), rows), cut],
            dst_ref=arrived.at[owner, :, cut],
            send_sem=score_send_sem.at[target, c],
            recv_sem=score_recv_sem.at[owner, c],
            device_id={"module": target // halves, "half": lax.rem(target, halves)},
            device_id_type=MESH,
        )

    def score_await(source, c):
        cut = pl.ds(c * chunk, chunk)
        return pltpu.make_async_remote_copy(
            src_ref=part.at[pl.ds(0, rows), cut],
            dst_ref=arrived.at[source, :, cut],
            send_sem=score_send_sem.at[source, c],
            recv_sem=score_recv_sem.at[source, c],
            device_id={"module": source // halves, "half": lax.rem(source, halves)},
            device_id_type=MESH,
        )

    for c in range(chunks):
        cut = slice(c * chunk, (c + 1) * chunk)

        def multiply(index):
            start = index * group_blocks
            lhs = blocks[pl.ds(start, group_blocks)].reshape(group_rows, blocks.shape[2])
            part[pl.ds(index * group_rows, group_rows), cut] = lax.dot_general(
                lhs, replay[cut, :], (((1,), (1,)), ((), ())), preferred_element_type=jnp.float32
            )

        if total == group_rows:
            multiply(0)
        else:
            pl.loop(0, total // group_rows)(multiply)
        for offset in range(1, owners):
            score_copy(lax.rem(owner + offset, owners), c).start()

    for c in range(chunks):
        cut = slice(c * chunk, (c + 1) * chunk)
        summed = part[pl.ds(pl.multiple_of(owner * rows, rows), rows), cut]
        for offset in range(1, owners):
            source = lax.rem(owner + offset, owners)
            score_await(source, c).wait_recv()
            summed = summed + arrived[source, :, cut]
        out_ref[:, cut] = summed

    def await_sent(offset):
        target = lax.rem(block + offset + 1, replays * modules)
        block_copy(lax.rem(target, modules), target // modules).wait_send()

    each(replays * modules - 1, await_sent)
    for c in range(chunks):
        for offset in range(1, owners):
            score_copy(lax.rem(owner + offset, owners), c).wait_send()


def body(
    replays,
    modules,
    halves,
    new_factors,
    new_counts,
    new_ids,
    replay_grads,
    replay_ids,
    slot_module,
    output_inverse,
    input_inverse,
):
    examples, _, _, width = new_factors.shape
    feat = width // 2
    columns, _, depth = replay_grads.shape
    share = depth // feat
    total = replays * modules * examples
    owners = modules * halves
    rows = total // owners
    chunk = 256 if columns % 256 == 0 else columns
    hbm = pl.BlockSpec(memory_space=pl.ANY)
    smem = pl.BlockSpec(memory_space=pltpu.SMEM)
    summed = pl.pallas_call(
        functools.partial(kernel, (replays, modules, halves, chunk)),
        out_shape=jax.ShapeDtypeStruct((rows, columns), jnp.float32),
        in_specs=[smem, smem, hbm, hbm, hbm, hbm],
        out_specs=pl.BlockSpec(memory_space=pltpu.VMEM),
        scratch_shapes=[
            pltpu.VMEM(new_factors.shape, jnp.bfloat16),
            pltpu.VMEM((columns, depth), jnp.bfloat16),
            pltpu.VMEM(output_inverse.shape, jnp.float32),
            pltpu.VMEM(input_inverse.shape, jnp.float32),
            pltpu.VMEM((examples * share, 2 * feat), jnp.float32),
            pltpu.VMEM((modules, examples, depth), jnp.bfloat16),
            pltpu.VMEM((replays * modules, examples, depth), jnp.bfloat16),
            pltpu.VMEM((total, columns), jnp.float32),
            pltpu.VMEM((owners, rows, columns), jnp.float32),
            pltpu.SemaphoreType.DMA((4,)),
            pltpu.SemaphoreType.DMA((replays * modules,)),
            pltpu.SemaphoreType.DMA((replays * modules,)),
            pltpu.SemaphoreType.DMA((owners, columns // chunk)),
            pltpu.SemaphoreType.DMA((owners, columns // chunk)),
        ],
        compiler_params=pltpu.CompilerParams(
            collective_id=0, has_side_effects=True, vmem_limit_bytes=60 * 1024 * 1024
        ),
        name="attribution",
    )(
        slot_module,
        new_counts,
        new_factors,
        replay_grads.reshape(columns, depth),
        output_inverse,
        input_inverse,
    )
    self_pairs = new_ids[:, None] == replay_ids[None, :]
    return jnp.where(self_pairs, jnp.zeros((), jnp.float32), summed)


def solution(mesh):
    in_specs = (
        P(("groups", "replay", "module"), None, None, None),
        P(("groups", "replay", "module")),
        P(("groups", "module", "half")),
        P(("groups", "replay"), "module", "half"),
        P(("groups", "replay")),
        P(),
        P(),
        P(),
    )
    out_specs = P(("groups", "module", "half"), "replay")
    return jax.shard_map(
        functools.partial(body, mesh.shape["replay"], mesh.shape["module"], mesh.shape["half"]),
        mesh=mesh,
        in_specs=in_specs,
        out_specs=out_specs,
        check_vma=False,
    )
```

time: 70.2 us -> 20.4 us (0.29)
  blocking collectives: 22.3 us -> 0 us
  waiting for transfers between devices: 20.1 us -> 0 us
  Pallas kernels: 0 us -> 18.7 us
  between operations: 13.5 us -> 0.03 us
  matrix products: 9.07 us -> 0 us
  other arithmetic: 3.53 us -> 1.49 us
  local copies, waits for them, and re-layouts: 1.37 us -> 0.01 us
    reduce_scatter x1 -> x0, waiting for transfers between devices: 20.1 us -> none  [body(): lax.psum_scatter(partials, ('module', 'half'), scatter_dimension=0, tiled...]
    pallas_call x0 -> x1, Pallas kernels: none -> 18.7 us  [body(): pl.pallas_call(functools.partial(kernel, (replays, modules, halves, chunk...]
    all_gather x1 -> x0, blocking collectives: 14.1 us -> none  [body(): lax.all_gather(new_block, 'replay', axis=0, tiled=True)]
    dot_general x7 -> x0, matrix products: 9.07 us -> none  [the longest x1 2.02 us: body(): jnp.einsum('estr,estc->esrc', output_grads, activations, preferred_elemen...]
    all_to_all x1 -> x0, blocking collectives: 8.16 us -> none  [body(): lax.all_to_all(local_rows, 'module', split_axis=1, concat_axis=0, tiled=T...]
    slice x1 -> x0, local copies, waits for them, and re-layouts: 1.18 us -> none  [body(): output_grads = slot_factors[:, :, :, feature_count:]]
    select_n x2 -> x1, other arithmetic: 2.65 us -> 1.49 us  [body(): return jnp.where(self_pairs, jnp.zeros((), jnp.float32), summed)]
    lt x1 -> x0, other arithmetic: 0.88 us -> none  [body(): token_live = token_index[None, :] < new_counts[:, None]]
  transfers between devices with their start and end apart: 1 -> 0, of which waited for: 1 -> 0; matrix products, arithmetic and copies ran while one was open for 0% -> 0% of each run, Pallas kernels for 0% -> 0%
where the time goes in v1:
time: 20.4 us; the launch traced here: 20.2 us
  Pallas kernels  18.7 us (92%)
  other arithmetic  1.49 us (7%)
    pallas_call x1, Pallas kernels, body(): pl.pallas_call(functools.partial(kernel, (replays, modules, halves, chunk...  18.7 us
    select_n x1, other arithmetic, body(): return jnp.where(self_pairs, jnp.zeros((), jnp.float32), summed)  1.49 us

profile of v1, /device:TPU:0, one launch (start us, length us, event | category | flops | bytes accessed | tf_op | source)
XLA Modules:
  0.0 20.2 jit_solution(3114976301727666108)
XLA Ops:
  0.0 0.0 copy-start
  0.0 0.0 copy-start.1
  0.0 18.7 %attribution.1 = f32[16,768]{1,0:T(8,128)} custom-call(s32[2]{0:T(128)} %slot_module.1, s32[8]{0:T(128)} %counts.1, bf16[8,2,64,128]{3,2,1,0:T(8,128)(2,1)} %factors_hbm.1, bf16[768,2048]{1,0:T(8,128)(2,1)} %bitcast.1, f32[2,64,64]{2,1,0:T(8,128)} %left_hbm.1, f32[2,64,64]{2,1,0:T(8,128)} %right_hbm.1), custom_call_target="tpu_custom_call" | custom-call | tf_op jit(solution)/shard_map/attribution/pallas_call | solution.py:267
  18.7 0.0 copy-done
  18.7 0.0 copy-done.1
  18.7 1.5 %compare_select_fusion = f32[16,768]{1,0:T(8,128)} fusion(f32[16,768]{1,0:T(8,128)} %attribution.1, s32[768]{0:T(1024)S(1)} %copy-done, s32[16]{0:T(128)S(1)} %copy-done.1), kind=kLoop, calls=%fused_computation | loop fusion | flops 24576 | bytes 101440 | tf_op jit(solution)/shard_map/jit(_where)/select_n | solution.py:301
Async XLA Ops:
  0.0 18.7 %copy-start = (s32[768]{0:T(1024)S(1)}, s32[768]{0:T(1024)}, u32[]{:S(2)}) copy-start(s32[768]{0:T(1024)} %param.12) | copy-start | bytes 9220
  0.0 18.7 %copy-start.1 = (s32[16]{0:T(128)S(1)}, s32[16]{0:T(128)}, u32[]{:S(2)}) copy-start(s32[16]{0:T(128)} %param.10) | copy-start | bytes 196

commit v2 on v1

--- a/solution.py
+++ b/solution.py
@@ -9,6 +9,8 @@
 
 MESH = pl.DeviceIdType.MESH
 UNROLL = 16
+EARLY = 1
+LATE = 2
 
 
 def each(count, step):
@@ -155,90 +157,141 @@
             device_id_type=MESH,
         )
 
-    for step in range(modules):
-        slot = lax.rem(x + 1 + step, modules)
+    for slot in range(modules):
         precondition(slot)
-        if step == 0:
-            pl.semaphore_wait(barrier, replays * modules - 1 + modules * (halves - 1))
-        first = 0 if step < modules - 1 else 1
-        each(replays - first, lambda index: block_copy(slot, lax.rem(z + first + index, replays)).start())
     blocks[block] = outgoing[x]
-
-    def await_block(offset):
-        source = lax.rem(block + offset + 1, replays * modules)
+    pl.semaphore_wait(barrier, replays * modules - 1 + modules * (halves - 1))
+
+    def neighbour(step):
+        if replays & (replays - 1):
+            return lax.rem(z + step, replays)
+        other, bit = z, 1
+        while bit < replays:
+            other = other + bit * ((step // bit) % 2) * (1 - 2 * ((z // bit) % 2))
+            bit *= 2
+        return other
+
+    def send_blocks(step):
+        for offset in range(1, modules):
+            block_copy(lax.rem(x + offset, modules), neighbour(step)).start()
+        if not (isinstance(step, int) and step == 0):
+            block_copy(x, neighbour(step)).start()
+
+    send_blocks(0)
+    each(replays - 1, lambda index: send_blocks(1 + (index + 1) % (replays - 1)))
+
+    per_owner = replays // owners
+    step_rows = modules * examples
+
+    def await_block(slot, source):
         pltpu.make_async_remote_copy(
             src_ref=outgoing.at[0],
             dst_ref=blocks.at[source],
             send_sem=send_sem.at[source],
             recv_sem=recv_sem.at[source],
-            device_id={"replay": source // modules, "module": lax.rem(source, modules)},
+            device_id={"replay": source // modules, "module": slot},
             device_id_type=MESH,
         ).wait_recv()
 
-    replay_load.wait()
-    each(replays * modules - 1, await_block)
-
-    total = replays * modules * examples
-    rows = total // owners
-    group_rows = min(total, 256)
-    group_blocks = group_rows // examples
-
-    def score_copy(target, c):
+    def score_copy(source, c):
+        cut = pl.ds(c * chunk, chunk)
+        target = source // per_owner
+        return pltpu.make_async_remote_copy(
+            src_ref=part.at[pl.ds(pl.multiple_of(source * step_rows, step_rows), step_rows), cut],
+            dst_ref=arrived.at[
+                owner, pl.ds(pl.multiple_of((source % per_owner) * step_rows, step_rows), step_rows), cut
+            ],
+            send_sem=score_send_sem.at[source, c],
+            recv_sem=score_recv_sem.at[owner, source % per_owner, c],
+            device_id={"module": target // halves, "half": target % halves},
+            device_id_type=MESH,
+        )
+
+    def score_await(source, inner, c):
         cut = pl.ds(c * chunk, chunk)
         return pltpu.make_async_remote_copy(
-            src_ref=part.at[pl.ds(pl.multiple_of(target * rows, rows), rows), cut],
-            dst_ref=arrived.at[owner, :, cut],
-            send_sem=score_send_sem.at[target, c],
-            recv_sem=score_recv_sem.at[owner, c],
-            device_id={"module": target // halves, "half": lax.rem(target, halves)},
-            device_id_type=MESH,
-        )
-
-    def score_await(source, c):
-        cut = pl.ds(c * chunk, chunk)
-        return pltpu.make_async_remote_copy(
-            src_ref=part.at[pl.ds(0, rows), cut],
-            dst_ref=arrived.at[source, :, cut],
-            send_sem=score_send_sem.at[source, c],
-            recv_sem=score_recv_sem.at[source, c],
-            device_id={"module": source // halves, "half": lax.rem(source, halves)},
-            device_id_type=MESH,
-        )
+            src_ref=part.at[pl.ds(0, step_rows), cut],
+            dst_ref=arrived.at[source, pl.ds(inner * step_rows, step_rows), cut],
+            send_sem=score_send_sem.at[0, c],
+            recv_sem=score_recv_sem.at[source, inner, c],
+            device_id={"module": source // halves, "half": source % halves},
+            device_id_type=MESH,
+        )
+
+    replay_load.wait()
+
+    def await_step(step):
+        source = neighbour(step)
+        for offset in range(1, modules):
+            slot = lax.rem(x + offset, modules)
+            await_block(slot, source * modules + slot)
+        if not (isinstance(step, int) and step == 0):
+            await_block(x, source * modules + x)
+
+    def score_steps(first, count, pieces):
+        sources = [neighbour(first + inner) for inner in range(count)]
+        lhs = jnp.concatenate(
+            [blocks[source * modules + slot] for source in sources for slot in range(modules)], axis=0
+        )
+        for piece in range(pieces):
+            span = columns // pieces
+            cut = slice(piece * span, (piece + 1) * span)
+            scores = lax.dot_general(
+                lhs, replay[cut, :], (((1,), (1,)), ((), ())), preferred_element_type=jnp.float32
+            )
+            for inner, source in enumerate(sources):
+                part[pl.ds(pl.multiple_of(source * step_rows, step_rows), step_rows), cut] = scores[
+                    inner * step_rows : (inner + 1) * step_rows
+                ]
+            for source in sources:
+
+                @pl.when(source // per_owner != owner)
+                def _():
+                    for c in range(piece * span // chunk, (piece + 1) * span // chunk):
+                        score_copy(source, c).start()
+
+    batch = 2 if replays % 2 == 0 else 1
+    for inner in range(batch):
+        await_step(inner)
+    score_steps(0, batch, EARLY)
+
+    def later(index):
+        for inner in range(batch):
+            await_step((index + 1) * batch + inner)
+        score_steps((index + 1) * batch, batch, LATE)
+
+    each(replays // batch - 1, later)
 
     for c in range(chunks):
         cut = slice(c * chunk, (c + 1) * chunk)
-
-        def multiply(index):
-            start = index * group_blocks
-            lhs = blocks[pl.ds(start, group_blocks)].reshape(group_rows, blocks.shape[2])
-            part[pl.ds(index * group_rows, group_rows), cut] = lax.dot_general(
-                lhs, replay[cut, :], (((1,), (1,)), ((), ())), preferred_element_type=jnp.float32
-            )
-
-        if total == group_rows:
-            multiply(0)
-        else:
-            pl.loop(0, total // group_rows)(multiply)
-        for offset in range(1, owners):
-            score_copy(lax.rem(owner + offset, owners), c).start()
-
-    for c in range(chunks):
-        cut = slice(c * chunk, (c + 1) * chunk)
-        summed = part[pl.ds(pl.multiple_of(owner * rows, rows), rows), cut]
-        for offset in range(1, owners):
-            source = lax.rem(owner + offset, owners)
-            score_await(source, c).wait_recv()
-            summed = summed + arrived[source, :, cut]
-        out_ref[:, cut] = summed
-
-    def await_sent(offset):
-        target = lax.rem(block + offset + 1, replays * modules)
-        block_copy(lax.rem(target, modules), target // modules).wait_send()
-
-    each(replays * modules - 1, await_sent)
-    for c in range(chunks):
-        for offset in range(1, owners):
-            score_copy(lax.rem(owner + offset, owners), c).wait_send()
+        for inner in range(per_owner):
+            span = pl.ds(inner * step_rows, step_rows)
+            first = owner * per_owner * step_rows + inner * step_rows
+            summed = part[pl.ds(pl.multiple_of(first, step_rows), step_rows), cut]
+            for offset in range(1, owners):
+                source = lax.rem(owner + offset, owners)
+                score_await(source, inner, c).wait_recv()
+                summed = summed + arrived[source, span, cut]
+            out_ref[span, cut] = summed
+
+    def await_sent(step):
+        source = neighbour(step)
+        for offset in range(1, modules):
+            block_copy(lax.rem(x + offset, modules), source).wait_send()
+        if not (isinstance(step, int) and step == 0):
+            block_copy(x, source).wait_send()
+
+        @pl.when(source // per_owner != owner)
+        def _():
+            for c in range(chunks):
+                score_copy(source, c).wait_send()
+
+    await_sent(0)
+    each(replays - 1, lambda index: await_sent(index + 1))
+
+
+def pin(array):
+    return pltpu.with_memory_space_constraint(array, pltpu.HBM)
 
 
 def body(
@@ -261,8 +314,8 @@
     total = replays * modules * examples
     owners = modules * halves
     rows = total // owners
-    chunk = 256 if columns % 256 == 0 else columns
-    hbm = pl.BlockSpec(memory_space=pl.ANY)
+    chunk = 384 if columns % 384 == 0 else columns // LATE
+    hbm = pl.BlockSpec(memory_space=pltpu.HBM)
     smem = pl.BlockSpec(memory_space=pltpu.SMEM)
     summed = pl.pallas_call(
         functools.partial(kernel, (replays, modules, halves, chunk)),
@@ -282,20 +335,20 @@
             pltpu.SemaphoreType.DMA((4,)),
             pltpu.SemaphoreType.DMA((replays * modules,)),
             pltpu.SemaphoreType.DMA((replays * modules,)),
-            pltpu.SemaphoreType.DMA((owners, columns // chunk)),
-            pltpu.SemaphoreType.DMA((owners, columns // chunk)),
+            pltpu.SemaphoreType.DMA((replays, columns // chunk)),
+            pltpu.SemaphoreType.DMA((owners, replays // owners, columns // chunk)),
         ],
         compiler_params=pltpu.CompilerParams(
-            collective_id=0, has_side_effects=True, vmem_limit_bytes=60 * 1024 * 1024
+            collective_id=0, has_side_effects=True, vmem_limit_bytes=24 * 1024 * 1024
         ),
         name="attribution",
     )(
         slot_module,
         new_counts,
-        new_factors,
-        replay_grads.reshape(columns, depth),
-        output_inverse,
-        input_inverse,
+        pin(new_factors),
+        pin(replay_grads.reshape(columns, depth)),
+        pin(output_inverse),
+        pin(input_inverse),
     )
     self_pairs = new_ids[:, None] == replay_ids[None, :]
     return jnp.where(self_pairs, jnp.zeros((), jnp.float32), summed)

time: 20.4 us -> 18.2 us (0.89)
  Pallas kernels: 18.7 us -> 16 us
  local copies, waits for them, and re-layouts: 0.01 us -> 1.33 us
  other arithmetic: 1.49 us -> 0.69 us
    pallas_call x1, Pallas kernels: 18.7 us -> 16 us  [body(): pl.pallas_call(functools.partial(kernel, (replays, modules, halves, chunk...]
    unnamed x4 -> x8, local copies, waits for them, and re-layouts: 0.01 us -> 1.33 us
    select_n x1, other arithmetic: 1.49 us -> 0.69 us  [body(): return jnp.where(self_pairs, jnp.zeros((), jnp.float32), summed)]
where the time goes in v2:
time: 18.2 us; the launch traced here: 18 us
  Pallas kernels  16 us (88%)
  local copies, waits for them, and re-layouts  1.33 us (7%)
  other arithmetic  0.69 us (4%)
    pallas_call x1, Pallas kernels, body(): pl.pallas_call(functools.partial(kernel, (replays, modules, halves, chunk...  16 us
    unnamed x8, local copies, waits for them, and re-layouts  1.33 us
    select_n x1, other arithmetic, body(): return jnp.where(self_pairs, jnp.zeros((), jnp.float32), summed)  0.69 us

profile of v2, /device:TPU:0, one launch (start us, length us, event | category | flops | bytes accessed | tf_op | source)
XLA Modules:
  0.0 18.0 jit_solution(6950532157765932498)
XLA Ops:
  0.0 0.0 copy-start.3
  0.0 0.0 copy-start
  0.0 0.7 %copy-done = s32[2]{0:T(128)S(1)} copy-done((s32[2]{0:T(128)S(1)}, s32[2]{0:T(128)}, u32[]{:S(2)}) %copy-start) | copy-done | bytes 32
  0.7 0.0 copy-start.1
  0.7 0.7 %copy-done.1 = s32[8]{0:T(128)S(1)} copy-done((s32[8]{0:T(128)S(1)}, s32[8]{0:T(128)}, u32[]{:S(2)}) %copy-start.1) | copy-done | bytes 56
  1.3 0.0 copy-start.2
  1.3 16.0 %attribution.1 = f32[16,768]{1,0:T(8,128)S(1)} custom-call(s32[2]{0:T(128)S(1)} %copy-done, s32[8]{0:T(128)S(1)} %copy-done.1, bf16[8,2,64,128]{3,2,1,0:T(8,128)(2,1)} %factors_hbm.1, bf16[768,2048]{1,0:T(8,128)(2,1)} %bitcast.1, f32[2,64,64]{2,1,0:T(8,128)} %left_hbm.1, f32[2,64,64]{2,1,0:T(8,128)} %right_hbm.1), custom_call_target="tpu_custom_call" | custom-call | tf_op jit(solution)/shard_map/attribution/pallas_call | solution.py:320
  17.3 0.0 copy-done.3
  17.3 0.0 copy-done.2
  17.3 0.7 %compare_select_fusion = f32[16,768]{1,0:T(8,128)} fusion(f32[16,768]{1,0:T(8,128)S(1)} %attribution.1, s32[768]{0:T(1024)S(1)} %copy-done.2, s32[16]{0:T(128)S(1)} %copy-done.3), kind=kLoop, calls=%fused_computation | loop fusion | flops 24576 | bytes 101440 | tf_op jit(solution)/shard_map/jit(_where)/select_n | solution.py:354
Async XLA Ops:
  0.0 17.3 %copy-start.3 = (s32[16]{0:T(128)S(1)}, s32[16]{0:T(128)}, u32[]{:S(2)}) copy-start(s32[16]{0:T(128)} %param.10) | copy-start | bytes 196
  0.0 0.7 %copy-start = (s32[2]{0:T(128)S(1)}, s32[2]{0:T(128)}, u32[]{:S(2)}) copy-start(s32[2]{0:T(128)} %slot_module.1) | copy-start | bytes 28
  0.7 0.7 %copy-start.1 = (s32[8]{0:T(128)S(1)}, s32[8]{0:T(128)}, u32[]{:S(2)}) copy-start(s32[8]{0:T(128)} %counts.1) | copy-start | bytes 100
  1.3 16.0 %copy-start.2 = (s32[768]{0:T(1024)S(1)}, s32[768]{0:T(1024)}, u32[]{:S(2)}) copy-start(s32[768]{0:T(1024)} %param.12) | copy-start | bytes 9220

commit v3 on v2

--- a/solution.py
+++ b/solution.py
@@ -33,13 +33,15 @@
 
 def kernel(
     sizes,
-    slot_module,
-    counts,
+    slot_module_hbm,
+    counts_hbm,
     factors_hbm,
     replay_hbm,
     left_hbm,
     right_hbm,
     out_ref,
+    slot_module,
+    counts,
     factors,
     replay,
     left,
@@ -66,16 +68,6 @@
     columns = replay.shape[0]
     chunks = columns // chunk
 
-    small_loads = [
-        pltpu.make_async_copy(factors_hbm, factors, load_sem.at[0]),
-        pltpu.make_async_copy(left_hbm, left, load_sem.at[1]),
-        pltpu.make_async_copy(right_hbm, right, load_sem.at[2]),
-    ]
-    for load in small_loads:
-        load.start()
-    replay_load = pltpu.make_async_copy(replay_hbm, replay, load_sem.at[3])
-    replay_load.start()
-
     barrier = pltpu.get_barrier_semaphore()
 
     def greet_block(offset):
@@ -99,6 +91,18 @@
     each(replays * modules - 1, greet_block)
     for offset in range(modules * (halves - 1)):
         greet_owner(offset)
+
+    small_loads = [
+        pltpu.make_async_copy(factors_hbm, factors, load_sem.at[0]),
+        pltpu.make_async_copy(left_hbm, left, load_sem.at[1]),
+        pltpu.make_async_copy(right_hbm, right, load_sem.at[2]),
+        pltpu.make_async_copy(slot_module_hbm, slot_module, load_sem.at[4]),
+        pltpu.make_async_copy(counts_hbm, counts, load_sem.at[5]),
+    ]
+    for load in small_loads:
+        load.start()
+    replay_load = pltpu.make_async_copy(replay_hbm, replay, load_sem.at[3])
+    replay_load.start()
 
     for load in small_loads:
         load.wait()
@@ -316,13 +320,14 @@
     rows = total // owners
     chunk = 384 if columns % 384 == 0 else columns // LATE
     hbm = pl.BlockSpec(memory_space=pltpu.HBM)
-    smem = pl.BlockSpec(memory_space=pltpu.SMEM)
     summed = pl.pallas_call(
         functools.partial(kernel, (replays, modules, halves, chunk)),
         out_shape=jax.ShapeDtypeStruct((rows, columns), jnp.float32),
-        in_specs=[smem, smem, hbm, hbm, hbm, hbm],
+        in_specs=[hbm] * 6,
         out_specs=pl.BlockSpec(memory_space=pltpu.VMEM),
         scratch_shapes=[
+            pltpu.SMEM(slot_module.shape, jnp.int32),
+            pltpu.SMEM(new_counts.shape, jnp.int32),
             pltpu.VMEM(new_factors.shape, jnp.bfloat16),
             pltpu.VMEM((columns, depth), jnp.bfloat16),
             pltpu.VMEM(output_inverse.shape, jnp.float32),
@@ -332,7 +337,7 @@
             pltpu.VMEM((replays * modules, examples, depth), jnp.bfloat16),
             pltpu.VMEM((total, columns), jnp.float32),
             pltpu.VMEM((owners, rows, columns), jnp.float32),
-            pltpu.SemaphoreType.DMA((4,)),
+            pltpu.SemaphoreType.DMA((6,)),
             pltpu.SemaphoreType.DMA((replays * modules,)),
             pltpu.SemaphoreType.DMA((replays * modules,)),
             pltpu.SemaphoreType.DMA((replays, columns // chunk)),
@@ -343,8 +348,8 @@
         ),
         name="attribution",
     )(
-        slot_module,
-        new_counts,
+        pin(slot_module),
+        pin(new_counts),
         pin(new_factors),
         pin(replay_grads.reshape(columns, depth)),
         pin(output_inverse),

time: 18.2 us -> 16.3 us (0.90)
  local copies, waits for them, and re-layouts: 1.33 us -> 0.01 us
  Pallas kernels: 16 us -> 15.4 us
    unnamed x8 -> x4, local copies, waits for them, and re-layouts: 1.33 us -> 0.01 us
    pallas_call x1, Pallas kernels: 16 us -> 15.4 us  [body(): pl.pallas_call(functools.partial(kernel, (replays, modules, halves, chunk...]
where the time goes in v3:
time: 16.3 us; the launch traced here: 16.1 us
  Pallas kernels  15.4 us (94%)
  other arithmetic  0.69 us (4%)
    pallas_call x1, Pallas kernels, body(): pl.pallas_call(functools.partial(kernel, (replays, modules, halves, chunk...  15.4 us
    select_n x1, other arithmetic, body(): return jnp.where(self_pairs, jnp.zeros((), jnp.float32), summed)  0.69 us

profile of v3, /device:TPU:0, one launch (start us, length us, event | category | flops | bytes accessed | tf_op | source)
XLA Modules:
  0.0 16.1 jit_solution(11520799467655670912)
XLA Ops:
  0.0 0.0 copy-start
  0.0 0.0 copy-start.1
  0.0 15.4 %attribution.1 = f32[16,768]{1,0:T(8,128)S(1)} custom-call(s32[2]{0:T(128)} %slot_module_hbm.1, s32[8]{0:T(128)} %counts_hbm.1, bf16[8,2,64,128]{3,2,1,0:T(8,128)(2,1)} %factors_hbm.1, bf16[768,2048]{1,0:T(8,128)(2,1)} %bitcast.1, f32[2,64,64]{2,1,0:T(8,128)} %left_hbm.1, f32[2,64,64]{2,1,0:T(8,128)} %right_hbm.1), custom_call_target="tpu_custom_call" | custom-call | tf_op jit(solution)/shard_map/attribution/pallas_call | solution.py:323
  15.4 0.0 copy-done
  15.4 0.0 copy-done.1
  15.4 0.7 %compare_select_fusion = f32[16,768]{1,0:T(8,128)} fusion(f32[16,768]{1,0:T(8,128)S(1)} %attribution.1, s32[768]{0:T(1024)S(1)} %copy-done, s32[16]{0:T(128)S(1)} %copy-done.1), kind=kLoop, calls=%fused_computation | loop fusion | flops 24576 | bytes 101440 | tf_op jit(solution)/shard_map/jit(_where)/select_n | solution.py:359
Async XLA Ops:
  0.0 15.4 %copy-start = (s32[768]{0:T(1024)S(1)}, s32[768]{0:T(1024)}, u32[]{:S(2)}) copy-start(s32[768]{0:T(1024)} %param.12) | copy-start | bytes 9220
  0.0 15.4 %copy-start.1 = (s32[16]{0:T(128)S(1)}, s32[16]{0:T(128)}, u32[]{:S(2)}) copy-start(s32[16]{0:T(128)} %param.10) | copy-start | bytes 196

commit v4 on v3

--- a/solution.py
+++ b/solution.py
@@ -102,7 +102,6 @@
     for load in small_loads:
         load.start()
     replay_load = pltpu.make_async_copy(replay_hbm, replay, load_sem.at[3])
-    replay_load.start()
 
     for load in small_loads:
         load.wait()
@@ -161,6 +160,7 @@
             device_id_type=MESH,
         )
 
+    replay_load.start()
     for slot in range(modules):
         precondition(slot)
     blocks[block] = outgoing[x]
@@ -181,8 +181,9 @@
         if not (isinstance(step, int) and step == 0):
             block_copy(x, neighbour(step)).start()
 
+    each(replays - 1, lambda index: send_blocks(1 + (index + 1) % (replays - 1)))
+
     send_blocks(0)
-    each(replays - 1, lambda index: send_blocks(1 + (index + 1) % (replays - 1)))
 
     per_owner = replays // owners
     step_rows = modules * examples

time: 16.3 us -> 16.3 us (level)
  no operation moved by 1% of the time
where the time goes in v4:
time: 16.3 us; the launch traced here: 16.1 us
  Pallas kernels  15.4 us (94%)
  other arithmetic  0.69 us (4%)
    pallas_call x1, Pallas kernels, body(): pl.pallas_call(functools.partial(kernel, (replays, modules, halves, chunk...  15.4 us
    select_n x1, other arithmetic, body(): return jnp.where(self_pairs, jnp.zeros((), jnp.float32), summed)  0.69 us

profile of v4, /device:TPU:0, one launch (start us, length us, event | category | flops | bytes accessed | tf_op | source)
XLA Modules:
  0.0 16.1 jit_solution(14811732511474400636)
XLA Ops:
  0.0 0.0 copy-start
  0.0 0.0 copy-start.1
  0.0 15.4 %attribution.1 = f32[16,768]{1,0:T(8,128)S(1)} custom-call(s32[2]{0:T(128)} %slot_module_hbm.1, s32[8]{0:T(128)} %counts_hbm.1, bf16[8,2,64,128]{3,2,1,0:T(8,128)(2,1)} %factors_hbm.1, bf16[768,2048]{1,0:T(8,128)(2,1)} %bitcast.1, f32[2,64,64]{2,1,0:T(8,128)} %left_hbm.1, f32[2,64,64]{2,1,0:T(8,128)} %right_hbm.1), custom_call_target="tpu_custom_call" | custom-call | tf_op jit(solution)/shard_map/attribution/pallas_call | solution.py:324
  15.4 0.0 copy-done
  15.4 0.0 copy-done.1
  15.4 0.7 %compare_select_fusion = f32[16,768]{1,0:T(8,128)} fusion(f32[16,768]{1,0:T(8,128)S(1)} %attribution.1, s32[768]{0:T(1024)S(1)} %copy-done, s32[16]{0:T(128)S(1)} %copy-done.1), kind=kLoop, calls=%fused_computation | loop fusion | flops 24576 | bytes 101440 | tf_op jit(solution)/shard_map/jit(_where)/select_n | solution.py:360
Async XLA Ops:
  0.0 15.4 %copy-start = (s32[768]{0:T(1024)S(1)}, s32[768]{0:T(1024)}, u32[]{:S(2)}) copy-start(s32[768]{0:T(1024)} %param.12) | copy-start | bytes 9220
  0.0 15.4 %copy-start.1 = (s32[16]{0:T(128)S(1)}, s32[16]{0:T(128)}, u32[]{:S(2)}) copy-start(s32[16]{0:T(128)} %param.10) | copy-start | bytes 196
